TPU v7x, 32 devices: a whole 2x2x4 slice. The times are simulated.
32 devices in a mesh: member: 4 (over x, core), tile: 4 (over z), grp: 2 (over y).
Axes of the slice: x: 2, y: 2, z: 4, core: 2. Of those that a mesh axis runs over, the one named last changes fastest.
Arguments:
- members: float32 [80, 128, 1024], P(('member', 'grp'), 'tile'), may hold values from -6 to 6
- courant_x: float32 [128, 1024], P('tile'), may hold values from -0.48 to 0.48
- courant_y: float32 [128, 1024], P('tile'), may hold values from -0.48 to 0.48
- obs_cell: int32 [4, 8, 1024], P('tile', ('member', 'grp')), may hold values from 0 to 4095
- innovation: float32 [4, 8, 1024], P('tile', ('member', 'grp')), may hold values from -6 to 6
- obs_weight: float32 [4, 8, 1024], P('tile', ('member', 'grp')), may hold values from 0.5 to 3
- stencil_offsets: int32 [9, 2], replicated, may hold values from -2 to 2, as said below
- stencil_weights: float32 [9], replicated, may hold values from 0.2 to 1
Outputs:
- analysis: float32 [80, 128, 1024], P(('member', 'grp'), 'tile')
- increment: float32 [128, 1024], P('tile', ('member', 'grp'))
Inputs may be any that keep to these rules, and one draw needn't show every extreme that they name: `stencil_offsets`: each row is a stencil entry's offsets along rows and columns; some entry reaches 2 cells along rows and some along columns. `obs_cell`: cells of a block are numbered row by row, 128 to a row.
All inputs are finite; a program needn't handle non-finite values.
Results may differ from a plain program's by a relative error of at most 0.0001.
Values sent between devices are 32-bit elements; how exact they have to be, the bound alone decides.
A program may use at most 128 MiB of HBM per device.

v0:
```python
import math

import jax
import jax.numpy as jnp
from jax import lax
from jax.sharding import PartitionSpec as P

RADIUS = 2
FSTEPS = 3
STEP_SIZE = 0.25
GROUP = ("member", "grp")


def halo(cells, axis, width, dim):
    count = lax.axis_size(axis)
    head = lax.slice_in_dim(cells, 0, width, axis=dim)
    tail = lax.slice_in_dim(cells, cells.shape[dim] - width, cells.shape[dim], axis=dim)
    above = lax.ppermute(tail, axis, [(i, i + 1) for i in range(count - 1)])
    below = lax.ppermute(head, axis, [(i + 1, i) for i in range(count - 1)])
    return jnp.concatenate([above, cells, below], axis=dim)


def upwind(q, cx, cy):
    rows = q.shape[1]
    c = q[:, 1:-1]
    left = jnp.pad(c, ((0, 0), (0, 0), (1, 0)))[:, :, :-1]
    right = jnp.pad(c, ((0, 0), (0, 0), (0, 1)))[:, :, 1:]
    return (
        c
        - jnp.maximum(cx, 0.0) * (c - q[:, : rows - 2])
        - jnp.minimum(cx, 0.0) * (q[:, 2:] - c)
        - jnp.maximum(cy, 0.0) * (c - left)
        - jnp.minimum(cy, 0.0) * (right - c)
    )


def spread_out(f, taps, sign):
    rows = f.shape[1] - 2 * RADIUS
    cols = f.shape[2]
    g = jnp.pad(f, ((0, 0), (0, 0), (RADIUS, RADIUS)))
    total = 0.0
    for r in range(-RADIUS, RADIUS + 1):
        for c in range(-RADIUS, RADIUS + 1):
            part = g[:, RADIUS + sign * r : RADIUS + sign * r + rows, RADIUS + sign * c : RADIUS + sign * c + cols]
            total = total + taps[r + RADIUS, c + RADIUS] * part
    return total


def on_device(members, courant_x, courant_y, obs_cell, innovation, obs_weight, offsets, weights):
    n, rows, cols = members.shape
    reach = 2 * RADIUS
    edge = reach + FSTEPS
    groups = lax.axis_size(GROUP)
    total = n * groups
    tile = lax.axis_index("tile")
    tiles = lax.axis_size("tile")

    packed = halo(jnp.concatenate([members, courant_x[None], courant_y[None]]), "tile", edge, 1)
    q, cx, cy = packed[:n], packed[n], packed[n + 1]
    for s in range(FSTEPS):
        lo, hi = s + 1, rows + 2 * edge - s - 1
        q = upwind(q, cx[lo:hi], cy[lo:hi])
    fields = q[:, reach : reach + rows]

    own = jnp.sum(q, axis=0) / n
    mean = lax.psum(own, GROUP) / groups
    dev = (q - own[None]) / math.sqrt(total - 1)
    shift = (own - mean) * math.sqrt(n / (total - 1))
    ones = jnp.full_like(own, 1.0 / math.sqrt(groups))
    dev = jnp.concatenate([dev, shift[None], ones[None]])

    kr = jnp.arange(-RADIUS, RADIUS + 1)
    hit = (offsets[:, 0][:, None, None] == kr[None, :, None]) & (offsets[:, 1][:, None, None] == kr[None, None, :])
    taps = jnp.sum(jnp.where(hit, weights[:, None, None], 0.0), axis=0) / jnp.sum(weights)

    at = jnp.arange(rows + 2 * RADIUS) - RADIUS + tile * rows
    inside = ((at >= 0) & (at < tiles * rows)).astype(jnp.float32)[None, :, None]

    def apply(h):
        z = spread_out(dev * h[None], taps, -1) * inside
        y = spread_out(z, taps, 1)
        return jnp.sum(dev[:, reach : reach + rows] * y, axis=0) * -STEP_SIZE

    width = cols // groups
    cell = obs_cell.reshape(-1)
    w = obs_weight.reshape(-1)
    wi = w * innovation.reshape(-1)
    pick_r = (cell[None] // width == jnp.arange(rows)[:, None]).astype(jnp.float32)
    pick_c = (cell[:, None] % width == jnp.arange(width)[None]).astype(jnp.float32)
    both = jnp.dot(
        jnp.concatenate([pick_r * w[None], pick_r * wi[None]]), pick_c, precision=lax.Precision.HIGHEST
    )
    dense_w, dense_wi = both[:rows], both[rows:]

    def gathered(block):
        return halo(lax.all_gather(block, GROUP, axis=1, tiled=True), "tile", reach, 0)

    x0 = lax.psum_scatter(apply(gathered(-dense_wi)), GROUP, scatter_dimension=1, tiled=True)
    g1 = dense_w * x0 - dense_wi
    x1 = lax.psum_scatter(apply(gathered(g1)), GROUP, scatter_dimension=1, tiled=True)
    block = (1.0 - STEP_SIZE) * x0 + x1
    full = lax.all_gather(block, GROUP, axis=1, tiled=True)
    return fields + full[None], block


def solution(mesh):
    placed = (
        P(GROUP, "tile", None),
        P("tile", None),
        P("tile", None),
        P("tile", GROUP, None),
        P("tile", GROUP, None),
        P("tile", GROUP, None),
        P(),
        P(),
    )
    return jax.shard_map(
        on_device,
        mesh=mesh,
        in_specs=placed,
        out_specs=(P(GROUP, "tile", None), P("tile", GROUP)),
        check_vma=False,
    )
```

profile of v0, /device:TPU:0, one launch (start us, length us, event | category | flops | bytes accessed | tf_op | source)
XLA Modules:
  0.0 333.4 jit_solution(7404053742297085599)
XLA Ops:
  9.9 14.8 %all_gather.9 = f32[32,1024]{1,0:T(8,128)S(1)} all-gather(f32[32,128]{1,0:T(8,128)S(1)} %slice_negate_fusion), channel_id=1, replica_groups=mesh['member'=4,'tile'=4,'grp'=2] {'member','grp'}, dimensions={1}, use_global_device_ids=true | all-gather | bytes 147456 | tf_op jit(solution)/shard_map/all_gather | solution.py:96
  25.3 3.5 %collective-permute-start.2 = (f32[4,1024]{1,0:T(4,128)S(1)}, f32[4,1024]{1,0:T(4,128)S(1)}, u32[]{:S(2)}, u32[]{:S(2)}) collective-permute-start(f32[4,1024]{1,0:T(4,128)S(1)} %get-tuple-element.28), channel_id=1, source_target_pairs={{0,2},{2,4},{4,6},{1,3},{3,5},{5,7},{8,10},{10,12},{12,14},{9,11},... | collective-permute-start | bytes 49160 | tf_op jit(solution)/shard_map/ppermute | solution.py:18
  28.8 1.3 collective-permute-start.3
  31.3 4.6 %collective-permute-start = (f32[12,7,1024]{2,1,0:T(8,128)S(1)}, f32[12,7,1024]{2,1,0:T(8,128)S(1)}, u32[]{:S(2)}, u32[]{:S(2)}) collective-permute-start(f32[12,7,1024]{2,1,0:T(8,128)S(1)} %get-tuple-element.24), channel_id=1, source_target_pairs={{0,2},{2,4},{4,6},{1,3},{3,5},{5,7},{8,10},{10,12},{12,14},{9,11},... | collective-permute-start | bytes 1032200 | tf_op jit(solution)/shard_map/ppermute | solution.py:18
  35.9 1.3 collective-permute-start.1
  40.1 4.6 %collective-permute-done = f32[12,7,1024]{2,1,0:T(8,128)S(1)} collective-permute-done((f32[12,7,1024]{2,1,0:T(8,128)S(1)}, f32[12,7,1024]{2,1,0:T(8,128)S(1)}, u32[]{:S(2)}, u32[]{:S(2)}) %collective-permute-start) | collective-permute-done | bytes 344096 | tf_op jit(solution)/shard_map/ppermute | solution.py:18
  44.8 4.1 %collective-permute-done.1 = f32[12,7,1024]{2,1,0:T(8,128)S(1)} collective-permute-done((f32[12,7,1024]{2,1,0:T(8,128)S(1)}, f32[12,7,1024]{2,1,0:T(8,128)S(1)}, u32[]{:S(2)}, u32[]{:S(2)}) %collective-permute-start.1) | collective-permute-done | bytes 344096 | tf_op jit(solution)/shard_map/ppermute | solution.py:19
  49.8 1.5 fusion.93
  51.8 1.5 fusion.99
  57.8 54.3 %all-reduce.12.cloned.1.call-done = f32[40,1024]{1,0:T(8,128)} async-done(((f32[40,1024]{1,0:T(8,128)}), f32[40,1024]{1,0:T(8,128)}) %all-reduce.12.cloned.1.call-update) | async-done | bytes 163856 | tf_op jit(solution)/shard_map/psum | solution.py:66
  113.1 1.7 maximum_maximum_fusion
  114.8 26.1 %fusion.44 = f32[12,36,1024]{2,1,0:T(8,128)S(1)} fusion(f32[12,40,1024]{2,1,0:T(8,128)S(1)} %get-tuple-element.23, f32[36]{0:T(128)S(1)} %and_convert_fusion, f32[]{:T(128)} %bitcast.44, f32[]{:T(128)} %bitcast.43, f32[]{:T(128)} %bitcast.42, f32[]{:T(128)} %bitcast.41, f32[]{:T(128)} %bitcast.40, f32[]{:T(128)} %bitcast.39, f32[]{:T(128)} %bitcast.38, ...), kind=kLoop, calls=%fused_computation.129 | loop fusion | flops 22118400 | bytes 13566564 | tf_op jit(solution)/shard_map/mul | solution.py:80
  140.9 25.1 %fusion.164 = f32[32,1024]{1,0:T(8,128)S(1)} fusion(f32[12,36,1024]{2,1,0:T(8,128)S(1)} %fusion.44, f32[12,40,1024]{2,1,0:T(8,128)} %get-tuple-element.22, f32[]{:T(128)} %bitcast.44, f32[]{:T(128)} %bitcast.43, f32[]{:T(128)} %bitcast.42, f32[]{:T(128)} %bitcast.41, f32[]{:T(128)} %bitcast.40, f32[]{:T(128)} %bitcast.39, f32[]{:T(128)} %bitcast.38, ...), kind=kLoop, calls=%fused_computation.269 | loop fusion | flops 20021248 | bytes 11534436 | tf_op jit(solution)/shard_map/reduce_sum | solution.py:82
  166.7 34.4 %reduce-scatter.3.cloned.1.call-done = f32[32,128]{1,0:T(8,128)} async-done(((f32[32,1024]{1,0:T(8,128)}), f32[32,128]{1,0:T(8,128)}) %reduce-scatter.3.cloned.1.call-update) | async-done | bytes 16400 | tf_op jit(solution)/shard_map/reduce_scatter | solution.py:98
  201.9 12.9 %all_gather.10 = f32[32,1024]{1,0:T(8,128)S(1)} all-gather(f32[32,128]{1,0:T(8,128)S(1)} %fusion.219), channel_id=1, replica_groups=mesh['member'=4,'tile'=4,'grp'=2] {'member','grp'}, dimensions={1}, use_global_device_ids=true | all-gather | bytes 147456 | tf_op jit(solution)/shard_map/all_gather | solution.py:96
  214.8 3.4 %collective-permute-start.4 = (f32[4,1024]{1,0:T(4,128)S(1)}, f32[4,1024]{1,0:T(4,128)S(1)}, u32[]{:S(2)}, u32[]{:S(2)}) collective-permute-start(f32[4,1024]{1,0:T(4,128)S(1)} %get-tuple-element.26), channel_id=1, source_target_pairs={{0,2},{2,4},{4,6},{1,3},{3,5},{5,7},{8,10},{10,12},{12,14},{9,11},... | collective-permute-start | bytes 49160 | tf_op jit(solution)/shard_map/ppermute | solution.py:18
  218.2 1.5 collective-permute-start.5
  219.7 4.2 %collective-permute-done.5 = f32[4,1024]{1,0:T(4,128)S(1)} collective-permute-done((f32[4,1024]{1,0:T(4,128)S(1)}, f32[4,1024]{1,0:T(4,128)S(1)}, u32[]{:S(2)}, u32[]{:S(2)}) %collective-permute-start.5) | collective-permute-done | bytes 16416 | tf_op jit(solution)/shard_map/ppermute | solution.py:19
  224.0 1.7 broadcast_multiply_fusion
  225.8 26.2 %fusion.89 = f32[12,36,1024]{2,1,0:T(8,128)S(1)} fusion(f32[12,40,1024]{2,1,0:T(8,128)S(1)} %broadcast_multiply_fusion, f32[36]{0:T(128)S(1)} %and_convert_fusion, f32[]{:T(128)} %bitcast.44, f32[]{:T(128)} %bitcast.43, f32[]{:T(128)} %bitcast.42, f32[]{:T(128)} %bitcast.41, f32[]{:T(128)} %bitcast.40, f32[]{:T(128)} %bitcast.39, f32[]{:T(128)} %bitcast.38, ...), kind=kLoop, calls=%fused_computation.174 | loop fusion | flops 22118400 | bytes 13566564 | tf_op jit(solution)/shard_map/mul | solution.py:80
  251.9 25.1 %fusion.210 = f32[32,1024]{1,0:T(8,128)S(1)} fusion(f32[12,36,1024]{2,1,0:T(8,128)S(1)} %fusion.89, f32[12,40,1024]{2,1,0:T(8,128)} %get-tuple-element.22, f32[]{:T(128)} %bitcast.44, f32[]{:T(128)} %bitcast.43, f32[]{:T(128)} %bitcast.42, f32[]{:T(128)} %bitcast.41, f32[]{:T(128)} %bitcast.40, f32[]{:T(128)} %bitcast.39, f32[]{:T(128)} %bitcast.38, ...), kind=kLoop, calls=%fused_computation.315 | loop fusion | flops 20021248 | bytes 11534436 | tf_op jit(solution)/shard_map/reduce_sum | solution.py:82
  277.7 32.8 %reduce-scatter.5.cloned.1.call-done = f32[32,128]{1,0:T(8,128)} async-done(((f32[32,1024]{1,0:T(8,128)}), f32[32,128]{1,0:T(8,128)}) %reduce-scatter.5.cloned.1.call-update) | async-done | bytes 16400 | tf_op jit(solution)/shard_map/reduce_scatter | solution.py:100
  311.2 12.9 %all_gather.11 = f32[32,1024]{1,0:T(8,128)S(1)} all-gather(f32[32,128]{1,0:T(8,128)S(1)} %multiply_add_fusion), channel_id=1, replica_groups=mesh['member'=4,'tile'=4,'grp'=2] {'member','grp'}, dimensions={1}, use_global_device_ids=true | all-gather | bytes 147456 | tf_op jit(solution)/shard_map/all_gather | solution.py:102
  324.1 2.7 slice_add_fusion
  (71 shorter events, 17.0 us)
Async XLA Ops:
  7.2 41.7 %copy-start = (f32[10,32,1024]{2,1,0:T(8,128)S(1)}, f32[10,32,1024]{2,1,0:T(8,128)}, u32[]{:S(2)}) copy-start(f32[10,32,1024]{2,1,0:T(8,128)} %param.8) | copy-start | bytes 3932164
  7.2 41.7 %copy-start.3 = (f32[32,1024]{1,0:T(8,128)S(1)}, f32[32,1024]{1,0:T(8,128)}, u32[]{:S(2)}) copy-start(f32[32,1024]{1,0:T(8,128)} %param.10) | copy-start | bytes 393220
  7.2 41.7 %copy-start.4 = (f32[32,1024]{1,0:T(8,128)S(1)}, f32[32,1024]{1,0:T(8,128)}, u32[]{:S(2)}) copy-start(f32[32,1024]{1,0:T(8,128)} %param.9) | copy-start | bytes 393220
  7.2 30.0 %copy-start.10 = (s32[9,2]{0,1:T(2,128)S(1)}, s32[9,2]{0,1:T(2,128)}, u32[]{:S(2)}) copy-start(s32[9,2]{0,1:T(2,128)} %param.14) | copy-start | bytes 220
  7.2 30.0 %copy-start.11 = (f32[9]{0:T(128)S(1)}, f32[9]{0:T(128)}, u32[]{:S(2)}) copy-start(f32[9]{0:T(128)} %param.15) | copy-start | bytes 112
  24.6 0.7 copy-start.7
  25.3 31.5 %collective-permute-start.2 = (f32[4,1024]{1,0:T(4,128)S(1)}, f32[4,1024]{1,0:T(4,128)S(1)}, u32[]{:S(2)}, u32[]{:S(2)}) collective-permute-start(f32[4,1024]{1,0:T(4,128)S(1)} %get-tuple-element.28), channel_id=1, source_target_pairs={{0,2},{2,4},{4,6},{1,3},{3,5},{5,7},{8,10},{10,12},{12,14},{9,11},... | collective-permute-start | bytes 49160 | tf_op jit(solution)/shard_map/ppermute | solution.py:18
  28.8 28.1 %collective-permute-start.3 = (f32[4,1024]{1,0:T(4,128)S(1)}, f32[4,1024]{1,0:T(4,128)S(1)}, u32[]{:S(2)}, u32[]{:S(2)}) collective-permute-start(f32[4,1024]{1,0:T(4,128)S(1)} %get-tuple-element.29), channel_id=1, source_target_pairs={{2,0},{4,2},{6,4},{3,1},{5,3},{7,5},{10,8},{12,10},{14,12},{11,9},... | collective-permute-start | bytes 49160 | tf_op jit(solution)/shard_map/ppermute | solution.py:19
  31.3 13.5 %collective-permute-start = (f32[12,7,1024]{2,1,0:T(8,128)S(1)}, f32[12,7,1024]{2,1,0:T(8,128)S(1)}, u32[]{:S(2)}, u32[]{:S(2)}) collective-permute-start(f32[12,7,1024]{2,1,0:T(8,128)S(1)} %get-tuple-element.24), channel_id=1, source_target_pairs={{0,2},{2,4},{4,6},{1,3},{3,5},{5,7},{8,10},{10,12},{12,14},{9,11},... | collective-permute-start | bytes 1032200 | tf_op jit(solution)/shard_map/ppermute | solution.py:18
  35.9 13.0 %collective-permute-start.1 = (f32[12,7,1024]{2,1,0:T(8,128)S(1)}, f32[12,7,1024]{2,1,0:T(8,128)S(1)}, u32[]{:S(2)}, u32[]{:S(2)}) collective-permute-start(f32[12,7,1024]{2,1,0:T(8,128)S(1)} %get-tuple-element.25), channel_id=1, source_target_pairs={{2,0},{4,2},{6,4},{3,1},{5,3},{7,5},{10,8},{12,10},{14,12},{11,9},... | collective-permute-start | bytes 1032200 | tf_op jit(solution)/shard_map/ppermute | solution.py:19
  54.8 0.7 copy-start.6
  54.8 1.7 copy-start.2
  55.5 0.7 copy-start.5
  55.8 58.9 %copy-start.1 = (f32[10,40,1024]{2,1,0:T(8,128)}, f32[10,40,1024]{2,1,0:T(8,128)S(1)}, u32[]{:S(2)}) copy-start(f32[10,40,1024]{2,1,0:T(8,128)S(1)} %subtract_multiply_fusion) | copy-start | bytes 4915204
  55.9 56.2 %all-reduce.12.cloned.1.call-start = ((), (), s32[]{:S(2)}) async-start(), calls=%async_computation.2 | async-start | bytes 327680 | tf_op jit(solution)/shard_map/psum | solution.py:66
  56.6 144.5 %reduce-scatter.3.cloned.1.call-start = ((), (), s32[]{:S(2)}) async-start(), calls=%async_computation.3 | async-start | bytes 147456 | tf_op jit(solution)/shard_map/reduce_scatter | solution.py:98
  166.7 143.8 %reduce-scatter.5.cloned.1.call-start = ((), (), s32[]{:S(2)}) async-start(), calls=%async_computation.4 | async-start | bytes 147456 | tf_op jit(solution)/shard_map/reduce_scatter | solution.py:100
  214.8 4.9 %collective-permute-start.4 = (f32[4,1024]{1,0:T(4,128)S(1)}, f32[4,1024]{1,0:T(4,128)S(1)}, u32[]{:S(2)}, u32[]{:S(2)}) collective-permute-start(f32[4,1024]{1,0:T(4,128)S(1)} %get-tuple-element.26), channel_id=1, source_target_pairs={{0,2},{2,4},{4,6},{1,3},{3,5},{5,7},{8,10},{10,12},{12,14},{9,11},... | collective-permute-start | bytes 49160 | tf_op jit(solution)/shard_map/ppermute | solution.py:18
  218.2 5.8 %collective-permute-start.5 = (f32[4,1024]{1,0:T(4,128)S(1)}, f32[4,1024]{1,0:T(4,128)S(1)}, u32[]{:S(2)}, u32[]{:S(2)}) collective-permute-start(f32[4,1024]{1,0:T(4,128)S(1)} %get-tuple-element.27), channel_id=1, source_target_pairs={{2,0},{4,2},{6,4},{3,1},{5,3},{7,5},{10,8},{12,10},{14,12},{11,9},... | collective-permute-start | bytes 49160 | tf_op jit(solution)/shard_map/ppermute | solution.py:19
  251.9 58.5 %copy-start.9 = (f32[32,128]{1,0:T(8,128)S(1)}, f32[32,128]{1,0:T(8,128)}, u32[]{:S(2)}) copy-start(f32[32,128]{1,0:T(8,128)} %reduce-scatter.3.cloned.1.call-done) | copy-start | bytes 49156
  311.2 15.7 %copy-start.8 = (f32[32,128]{1,0:T(8,128)}, f32[32,128]{1,0:T(8,128)S(1)}, u32[]{:S(2)}) copy-start(f32[32,128]{1,0:T(8,128)S(1)} %multiply_add_fusion) | copy-start | bytes 49156
Sparse Core Ops, SparseCore 0:
  60.3 51.6 all-reduce.11
  166.8 34.3 reduce-scatter.2
  277.8 32.6 reduce-scatter.4
where the time goes:
time: 336 us; the launch traced here: 333 us
  waiting for transfers between devices  135 us (40%)
  other arithmetic  123 us (37%)
  blocking collectives  40.6 us (12%)
  starting transfers between devices  15.8 us (5%)
  between operations  14.1 us (4%)
  local copies, waits for them, and re-layouts  4.15 us (1%)
    psum x1, waiting for transfers between devices, on_device(): mean = lax.psum(own, GROUP) / groups  54.3 us
    mul x3, other arithmetic, apply(): z = spread_out(dev * h[None], taps, -1) * inside  54 us
    reduce_sum x2, other arithmetic, apply(): return jnp.sum(dev[:, reach:reach + rows] * y, axis=0) * -STEP_SIZE  50.1 us
    reduce_scatter x1, waiting for transfers between devices, on_device(): lax.psum_scatter(apply(gathered(-dense_wi)), GROUP, scatter_dimension=1,...  34.4 us
    reduce_scatter x1, waiting for transfers between devices, on_device(): lax.psum_scatter(apply(gathered(g1)), GROUP, scatter_dimension=1, tiled=T...  32.8 us
    all_gather x2, blocking collectives, gathered(): lax.all_gather(block, GROUP, axis=1, tiled=True)  27.7 us
    all_gather x1, blocking collectives, on_device(): full = lax.all_gather(block, GROUP, axis=1, tiled=True)  12.9 us
    ppermute x3, starting transfers between devices, halo(): above = lax.ppermute(tail, axis, [(i, i + 1) for i in range(count - 1)])  11.4 us
  transfers between devices with their start and end apart: 9, of which 6 were waited for; matrix products, arithmetic and copies ran while one was open for 3% of the time, Pallas kernels for 0%

commit v1 on v0

v1 whole, which is shorter than its diff:
```python
import functools
import math

import jax
import jax.numpy as jnp
from jax import lax
from jax.experimental import pallas as pl
from jax.experimental.pallas import tpu as pltpu
from jax.sharding import PartitionSpec as P

RADIUS = 2
FSTEPS = 3
STEP_SIZE = 0.25
GROUP = ("member", "grp")
MESH = pl.DeviceIdType.MESH
SUB = 8
LANES = 128
REACH = 2 * RADIUS
SHIFTS = tuple(range(-RADIUS, RADIUS + 1))


def remote(src, dst, send_sem, recv_sem, where):
    return pltpu.make_async_remote_copy(
        src_ref=src, dst_ref=dst, send_sem=send_sem, recv_sem=recv_sem, device_id=where, device_id_type=MESH
    )


def moved(blocks, c, lane):
    if c == 0:
        return blocks
    turned = [pltpu.roll(x, (-c) % LANES, 1) for x in blocks]
    nothing = jnp.zeros_like(blocks[0])
    out = []
    for b in range(len(blocks)):
        if c > 0:
            other = turned[b + 1] if b + 1 < len(blocks) else nothing
            out.append(jnp.where(lane >= LANES - c, other, turned[b]))
        else:
            other = turned[b - 1] if b > 0 else nothing
            out.append(jnp.where(lane < -c, other, turned[b]))
    return out


def kernel(
    shape,
    offs, wts, members, cx_hbm, cy_hbm, cell_ref, innov_ref, weight_ref,
    out_hbm, inc_ref,
    Q, C, T1, T2, D, OWN, MR, MB, MG, OBW, OBI, G0, G1,
    M0, U0, L0, M1, U1, L1, H, U, Z, ACC, XP, X0, R0, R1, NB, NM,
    in_sem, out_sem, hs, hr, s0, r0, s1, r1, sm1, rm1, sm2, rm2, sx0, rx0, sx1, rx1, sn, rn,
):
    n, rows, groups, n_grp = shape
    total = n * groups
    tiles = lax.axis_size("tile")
    tile = lax.axis_index("tile")
    me = lax.axis_index("member") * n_grp + lax.axis_index("grp")
    has_up = tile > 0
    has_down = tile < tiles - 1
    top = 2 * SUB
    tall = rows + 2 * REACH
    lane = lax.broadcasted_iota(jnp.int32, (SUB, LANES), 1)
    blocks = range(groups)

    def at(p, t=None):
        where = {"member": p // n_grp, "grp": lax.rem(p, n_grp)}
        if t is not None:
            where["tile"] = t
        return where

    def partner(d):
        return lax.rem(me + d, groups)

    def sender(d):
        return lax.rem(me + groups - d, groups)

    def loads():
        for b in blocks:
            cols = pl.ds(b * LANES, LANES)
            yield pltpu.make_async_copy(cx_hbm.at[:, cols], Q.at[n, b, pl.ds(top, rows)], in_sem.at[1, b])
            yield pltpu.make_async_copy(cy_hbm.at[:, cols], Q.at[n + 1, b, pl.ds(top, rows)], in_sem.at[2, b])
        for b in blocks:
            cols = pl.ds(b * LANES, LANES)
            yield pltpu.make_async_copy(members.at[:, :, cols], Q.at[pl.ds(0, n), b, pl.ds(top, rows)], in_sem.at[0, b])

    for copy in loads():
        copy.start()

    barrier = pltpu.get_barrier_semaphore()
    for d in range(1, groups):
        pl.semaphore_signal(barrier, inc=1, device_id=at(partner(d)), device_id_type=MESH)

    @pl.when(has_up)
    def _():
        for d in blocks:
            pl.semaphore_signal(barrier, inc=1, device_id=at(partner(d), tile - 1), device_id_type=MESH)

    @pl.when(has_down)
    def _():
        for d in blocks:
            pl.semaphore_signal(barrier, inc=1, device_id=at(partner(d), tile + 1), device_id_type=MESH)

    sides = jnp.where(has_up, 1, 0) + jnp.where(has_down, 1, 0)
    for m in range(3):
        @pl.when(sides == m)
        def _(m=m):
            pl.semaphore_wait(barrier, groups - 1 + m * groups)

    for copy in loads():
        copy.wait()

    def up_copy(k):
        return remote(
            Q.at[k, :, pl.ds(top, SUB)], Q.at[k, :, pl.ds(top + rows, SUB)], hs.at[0, k], hr.at[0, k],
            {"tile": tile - 1},
        )

    def down_copy(k):
        return remote(
            Q.at[k, :, pl.ds(top + rows - SUB, SUB)], Q.at[k, :, pl.ds(top - SUB, SUB)], hs.at[1, k], hr.at[1, k],
            {"tile": tile + 1},
        )

    order = [n, n + 1] + list(range(n))
    for k in order:
        @pl.when(has_up)
        def _(k=k):
            up_copy(k).start()

        @pl.when(has_down)
        def _(k=k):
            down_copy(k).start()

    def halo_wait(k):
        @pl.when(has_down)
        def _():
            up_copy(k).wait_recv()

        @pl.when(has_up)
        def _():
            down_copy(k).wait_recv()

    blank = jnp.zeros((SUB, LANES), jnp.float32)

    @pl.when(jnp.logical_not(has_up))
    def _():
        for k in range(n + 2):
            for b in blocks:
                Q[k, b, pl.ds(top - SUB, SUB)] = blank
        for b in blocks:
            U0[b] = blank
            U1[b] = blank

    @pl.when(jnp.logical_not(has_down))
    def _():
        for k in range(n + 2):
            for b in blocks:
                Q[k, b, pl.ds(top + rows, SUB)] = blank
        for b in blocks:
            L0[b] = blank
            L1[b] = blank

    def spread_start(src, main, up, low, ssem, rsem, edges):
        for d in range(1, groups):
            remote(src, main.at[me], ssem.at[0, d], rsem.at[0, d], at(partner(d))).start()
        if edges:
            @pl.when(has_up)
            def _():
                for d in blocks:
                    remote(src.at[pl.ds(0, SUB)], low.at[me], ssem.at[1, d], rsem.at[1, d], at(partner(d), tile - 1)).start()

            @pl.when(has_down)
            def _():
                for d in blocks:
                    remote(src.at[pl.ds(rows - SUB, SUB)], up.at[me], ssem.at[2, d], rsem.at[2, d], at(partner(d), tile + 1)).start()

    def spread_recv(src, main, up, low, ssem, rsem, edges):
        for d in range(1, groups):
            remote(src, main.at[sender(d)], ssem.at[0, d], rsem.at[0, d], at(sender(d))).wait_recv()
        if edges:
            @pl.when(has_down)
            def _():
                for d in blocks:
                    remote(src.at[pl.ds(0, SUB)], low.at[sender(d)], ssem.at[1, d], rsem.at[1, d], at(sender(d))).wait_recv()

            @pl.when(has_up)
            def _():
                for d in blocks:
                    remote(src.at[pl.ds(0, SUB)], up.at[sender(d)], ssem.at[2, d], rsem.at[2, d], at(sender(d))).wait_recv()

    def spread_sent(src, main, up, low, ssem, rsem, edges):
        for d in range(1, groups):
            remote(src, main.at[me], ssem.at[0, d], rsem.at[0, d], at(partner(d))).wait_send()
        if edges:
            @pl.when(has_up)
            def _():
                for d in blocks:
                    remote(src.at[pl.ds(0, SUB)], low.at[me], ssem.at[1, d], rsem.at[1, d], at(partner(d), tile - 1)).wait_send()

            @pl.when(has_down)
            def _():
                for d in blocks:
                    remote(src.at[pl.ds(0, SUB)], up.at[me], ssem.at[2, d], rsem.at[2, d], at(partner(d), tile + 1)).wait_send()

    def deal(src, dst, ssem, rsem):
        return [
            remote(src.at[partner(d)], dst.at[me], ssem.at[0, d], rsem.at[0, d], at(partner(d)))
            for d in range(1, groups)
        ]

    def dealt_wait(src, dst, ssem, rsem):
        for d in range(1, groups):
            remote(src.at[0], dst.at[sender(d)], ssem.at[0, d], rsem.at[0, d], at(sender(d))).wait_recv()

    cell = cell_ref[0]
    w = weight_ref[0]
    wi = -w * innov_ref[0]
    count = cell.shape[1]
    row_of = cell // LANES
    col_of = cell % LANES
    pick_r = lax.broadcasted_iota(jnp.int32, (rows, count), 0) == row_of
    pick_c = (lax.broadcasted_iota(jnp.int32, (LANES, count), 0) == col_of).astype(jnp.float32)
    left = jnp.concatenate([jnp.where(pick_r, w, 0.0), jnp.where(pick_r, wi, 0.0)], axis=0)
    both = lax.dot_general(
        left, pick_c, (((1,), (1,)), ((), ())),
        precision=lax.Precision.HIGHEST, preferred_element_type=jnp.float32,
    )
    OBW[...] = both[:rows]
    OBI[...] = both[rows:]
    G0[...] = both[rows:]
    M0[me] = both[rows:]
    spread0 = (G0, M0, U0, L0, s0, r0, True)
    spread_start(*spread0)

    halo_wait(n)
    halo_wait(n + 1)

    def coefficients(i, carry):
        r = pl.ds(pl.multiple_of(top - SUB + i * SUB, SUB), SUB)
        for b in blocks:
            cx = Q[n, b, r]
            cy = Q[n + 1, b, r]
            C[0, b, r] = 1.0 - jnp.abs(cx) - jnp.abs(cy)
            C[1, b, r] = jnp.maximum(cx, 0.0)
            C[2, b, r] = -jnp.minimum(cx, 0.0)
            C[3, b, r] = jnp.maximum(cy, 0.0)
            C[4, b, r] = -jnp.minimum(cy, 0.0)
        return carry

    lax.fori_loop(0, rows // SUB + 2, coefficients, 0)
    for i in range(tall // SUB):
        for b in blocks:
            OWN[b, pl.ds(i * SUB, SUB)] = blank

    def advect(get, first, i):
        base = first + i * SUB
        q = [get(b, base) for b in blocks]
        before = moved(q, -1, lane)
        after = moved(q, 1, lane)
        out = []
        for b in blocks:
            r = pl.ds(base, SUB)
            out.append(
                (C[0, b, r] * q[b] + C[1, b, r] * get(b, base - 1))
                + (C[2, b, r] * get(b, base + 1) + C[3, b, r] * before[b])
                + C[4, b, r] * after[b]
            )
        return out

    def forecast(k, carry):
        halo_wait(k)
        for i in range(rows // SUB + 2):
            new = advect(lambda b, r: Q[k, b, pl.ds(r, SUB)], top - SUB, i)
            for b in blocks:
                T1[b, pl.ds(top - SUB + i * SUB, SUB)] = new[b]
        for i in range(rows // SUB + 2):
            new = advect(lambda b, r: T1[b, pl.ds(r, SUB)], top - SUB, i)
            for b in blocks:
                T2[b, pl.ds(top - SUB + i * SUB, SUB)] = new[b]
        for i in range(tall // SUB):
            new = advect(lambda b, r: T2[b, pl.ds(r, SUB)], top - REACH, i)
            r = pl.ds(i * SUB, SUB)
            for b in blocks:
                D[k, b, r] = new[b]
                OWN[b, r] += new[b] * (1.0 / n)
        return carry

    lax.fori_loop(0, n, forecast, 0)

    mean_out = deal(OWN, MR, sm1, rm1)
    for copy in mean_out:
        copy.start()
    MR[me] = OWN[me]

    def centre(k, carry):
        for i in range(tall // SUB):
            r = pl.ds(i * SUB, SUB)
            for b in blocks:
                D[k, b, r] = D[k, b, r] - OWN[b, r]
        return carry

    lax.fori_loop(0, n, centre, 0)

    entries = offs.shape[0]
    weights = [wts[s] for s in range(entries)]
    weight_sum = weights[0]
    for s in range(1, entries):
        weight_sum = weight_sum + weights[s]
    inverse = 1.0 / jnp.full((SUB, LANES), weight_sum, jnp.float32)
    scale = inverse * inverse * (-STEP_SIZE / (total - 1))
    first_row = tile * rows - RADIUS
    end_row = tiles * rows
    sub = lax.broadcasted_iota(jnp.int32, (SUB, LANES), 0)

    def assemble(main, up, low):
        for b in blocks:
            H[b, pl.ds(0, REACH)] = up[b, pl.ds(SUB - REACH, REACH)]
            H[b, pl.ds(REACH, rows)] = main[b]
            H[b, pl.ds(REACH + rows, REACH)] = low[b, pl.ds(0, REACH)]

    def clear():
        for i in range(rows // SUB):
            for b in blocks:
                ACC[b, pl.ds(i * SUB, SUB)] = blank

    def apply(k, carry):
        def lift(i, c1):
            r = pl.ds(pl.multiple_of(i * SUB, SUB), SUB)
            u = [D[k, b, r] * H[b, r] for b in blocks]
            for c in SHIFTS:
                v = moved(u, c, lane)
                for b in blocks:
                    U[c + RADIUS, b, r] = v[b]
            return c1

        lax.fori_loop(0, tall // SUB, lift, 0)

        def adjoint(i, c1):
            z = []
            place = first_row + i * SUB + sub
            keep = (place >= 0) & (place < end_row)
            for b in blocks:
                acc = None
                for s in range(entries):
                    part = weights[s] * U[RADIUS - offs[s, 1], b, pl.ds(i * SUB + RADIUS - offs[s, 0], SUB)]
                    acc = part if acc is None else acc + part
                z.append(jnp.where(keep, acc, 0.0))
            r = pl.ds(pl.multiple_of(i * SUB, SUB), SUB)
            for c in SHIFTS:
                v = moved(z, c, lane)
                for b in blocks:
                    Z[c + RADIUS, b, r] = v[b]
            return c1

        lax.fori_loop(0, tall // SUB, adjoint, 0)

        def direct(i, c1):
            r = pl.ds(pl.multiple_of(i * SUB, SUB), SUB)
            for b in blocks:
                acc = None
                for s in range(entries):
                    part = weights[s] * Z[RADIUS + offs[s, 1], b, pl.ds(i * SUB + RADIUS + offs[s, 0], SUB)]
                    acc = part if acc is None else acc + part
                ACC[b, r] += D[k, b, pl.ds(i * SUB + REACH, SUB)] * acc
            return c1

        lax.fori_loop(0, rows // SUB, direct, 0)
        return carry

    def publish(copies, dst):
        for i in range(rows // SUB):
            r = pl.ds(i * SUB, SUB)
            for b in blocks:
                XP[b, r] = ACC[b, r] * scale
        for copy in copies:
            copy.start()
        dst[me] = XP[me]

    spread_recv(*spread0)
    assemble(M0, U0, L0)
    clear()
    half = n // 2
    lax.fori_loop(0, half, apply, 0)
    dealt_wait(OWN, MR, sm1, rm1)
    mean = MR[0]
    for b in range(1, groups):
        mean = mean + MR[b]
    MB[...] = mean * (1.0 / groups)
    MG[me] = mean * (1.0 / groups)
    spread_mean = (MB, MG, None, None, sm2, rm2, False)
    spread_start(*spread_mean)
    lax.fori_loop(half, n, apply, 0)
    spread_recv(*spread_mean)
    for b in blocks:
        D[n, b] = (OWN[b] - MG[b]) * math.sqrt(n)
        D[n + 1, b] = jnp.full((tall, LANES), math.sqrt((total - 1) / groups), jnp.float32)
    lax.fori_loop(n, n + 2, apply, 0)
    first_out = deal(XP, R0, sx0, rx0)
    publish(first_out, R0)
    dealt_wait(XP, R0, sx0, rx0)
    x0 = R0[0]
    for b in range(1, groups):
        x0 = x0 + R0[b]
    X0[...] = x0 * (1.0 - STEP_SIZE)
    g1 = OBW[...] * x0 + OBI[...]
    G1[...] = g1
    M1[me] = g1
    spread1 = (G1, M1, U1, L1, s1, r1, True)
    spread_start(*spread1)
    for copy in first_out:
        copy.wait_send()
    spread_recv(*spread1)
    assemble(M1, U1, L1)
    clear()
    lax.fori_loop(0, n + 2, apply, 0)
    second_out = deal(XP, R1, sx1, rx1)
    publish(second_out, R1)
    dealt_wait(XP, R1, sx1, rx1)
    block = X0[...]
    for b in blocks:
        block = block + R1[b]
    NB[...] = block
    NM[me] = block
    inc_ref[...] = block
    spread_last = (NB, NM, None, None, sn, rn, False)
    spread_start(*spread_last)

    for k in order:
        @pl.when(has_up)
        def _(k=k):
            up_copy(k).wait_send()

        @pl.when(has_down)
        def _(k=k):
            down_copy(k).wait_send()

    spread_recv(*spread_last)
    writes = []
    for b in blocks:
        base = OWN[b, pl.ds(REACH, rows)] + NM[b]

        def finish(k, carry, b=b, base=base):
            Q[k, b, pl.ds(top, rows)] = D[k, b, pl.ds(REACH, rows)] + base
            return carry

        lax.fori_loop(0, n, finish, 0)
        copy = pltpu.make_async_copy(
            Q.at[pl.ds(0, n), b, pl.ds(top, rows)], out_hbm.at[:, :, pl.ds(b * LANES, LANES)], out_sem.at[b]
        )
        copy.start()
        writes.append(copy)
    spread_sent(*spread0)
    for copy in mean_out + second_out:
        copy.wait_send()
    spread_sent(*spread_mean)
    spread_sent(*spread1)
    spread_sent(*spread_last)
    for copy in writes:
        copy.wait()


def on_device(members, courant_x, courant_y, obs_cell, innovation, obs_weight, offsets, weights):
    n, rows, cols = members.shape
    groups = lax.axis_size(GROUP)
    n_grp = lax.axis_size("grp")
    assert cols == groups * LANES and rows % SUB == 0
    tall = rows + 2 * REACH
    deep = rows + 4 * SUB
    f32 = jnp.float32
    vmem = pltpu.VMEM
    dma = pltpu.SemaphoreType.DMA
    scratch = [
        vmem((n + 2, groups, deep, LANES), f32),
        vmem((5, groups, deep, LANES), f32),
        vmem((groups, deep, LANES), f32),
        vmem((groups, deep, LANES), f32),
        vmem((n + 2, groups, tall, LANES), f32),
        vmem((groups, tall, LANES), f32),
        vmem((groups, tall, LANES), f32),
        vmem((tall, LANES), f32),
        vmem((groups, tall, LANES), f32),
    ]
    scratch += [vmem((rows, LANES), f32)] * 4
    for _ in range(2):
        scratch += [vmem((groups, rows, LANES), f32), vmem((groups, SUB, LANES), f32), vmem((groups, SUB, LANES), f32)]
    scratch += [
        vmem((groups, tall, LANES), f32),
        vmem((len(SHIFTS), groups, tall + SUB, LANES), f32),
        vmem((len(SHIFTS), groups, tall, LANES), f32),
        vmem((groups, rows, LANES), f32),
        vmem((groups, rows, LANES), f32),
        vmem((rows, LANES), f32),
        vmem((groups, rows, LANES), f32),
        vmem((groups, rows, LANES), f32),
        vmem((rows, LANES), f32),
        vmem((groups, rows, LANES), f32),
        dma((3, groups)),
        dma((groups,)),
        dma((2, n + 2)),
        dma((2, n + 2)),
        dma((3, groups)),
        dma((3, groups)),
        dma((3, groups)),
        dma((3, groups)),
    ]
    scratch += [dma((1, groups))] * 10
    whole = pl.BlockSpec(memory_space=pltpu.VMEM)
    scalar = pl.BlockSpec(memory_space=pltpu.SMEM)
    left = pl.BlockSpec(memory_space=pl.ANY)
    return pl.pallas_call(
        functools.partial(kernel, (n, rows, groups, n_grp)),
        out_shape=(
            jax.ShapeDtypeStruct(members.shape, f32),
            jax.ShapeDtypeStruct((rows, LANES), f32),
        ),
        in_specs=[scalar, scalar, left, left, left, whole, whole, whole],
        out_specs=(left, whole),
        scratch_shapes=scratch,
        compiler_params=pltpu.CompilerParams(collective_id=0, has_side_effects=True, vmem_limit_bytes=40 << 20),
        name="cycle",
    )(offsets, weights, members, courant_x, courant_y, obs_cell, innovation, obs_weight)


def solution(mesh):
    placed = (
        P(GROUP, "tile", None),
        P("tile", None),
        P("tile", None),
        P("tile", GROUP, None),
        P("tile", GROUP, None),
        P("tile", GROUP, None),
        P(),
        P(),
    )
    return jax.shard_map(
        on_device,
        mesh=mesh,
        in_specs=placed,
        out_specs=(P(GROUP, "tile", None), P("tile", GROUP)),
        check_vma=False,
    )
```

time: 336 us -> 75.5 us (0.22)
  waiting for transfers between devices: 135 us -> 0 us
  other arithmetic: 123 us -> 0 us
  Pallas kernels: 0 us -> 66.3 us
  blocking collectives: 40.6 us -> 0 us
  starting transfers between devices: 15.8 us -> 0 us
  between operations: 14.1 us -> 0.65 us
  local copies, waits for them, and re-layouts: 4.15 us -> 8.27 us
    reduce_scatter x2 -> x0, waiting for transfers between devices: 67.2 us -> none  [the longest x1 34.4 us: on_device(): lax.psum_scatter(apply(gathered(-dense_wi)), GROUP, scatter_dimension=1,...]
    pallas_call x0 -> x1, Pallas kernels: none -> 66.3 us  [on_device(): pl.pallas_call(functools.partial(kernel, (n, rows, groups, n_grp)), out_s...]
    mul x13 -> x0, other arithmetic: 57.1 us -> none  [the longest x3 54 us: apply(): z = spread_out(dev * h[None], taps, -1) * inside]
    psum x1 -> x0, waiting for transfers between devices: 54.3 us -> none  [on_device(): mean = lax.psum(own, GROUP) / groups]
    reduce_sum x5 -> x0, other arithmetic: 51.9 us -> none  [the longest x2 50.1 us: apply(): return jnp.sum(dev[:, reach:reach + rows] * y, axis=0) * -STEP_SIZE]
    all_gather x3 -> x0, blocking collectives: 40.6 us -> none  [the longest x2 27.7 us: gathered(): lax.all_gather(block, GROUP, axis=1, tiled=True)]
    ppermute x6 -> x0, starting transfers between devices: 15.5 us -> none  [the longest x3 11.4 us: halo(): above = lax.ppermute(tail, axis, [(i, i + 1) for i in range(count - 1)])]
    ppermute x6 -> x0, waiting for transfers between devices: 13 us -> none  [the longest x3 8.39 us: halo(): below = lax.ppermute(head, axis, [(i + 1, i) for i in range(count - 1)])]
  transfers between devices with their start and end apart: 9 -> 0, of which waited for: 6 -> 0; matrix products, arithmetic and copies ran while one was open for 3% -> 0% of each run, Pallas kernels for 0% -> 0%
where the time goes in v1:
time: 75.5 us; the launch traced here: 75.2 us
  Pallas kernels  66.3 us (88%)
  local copies, waits for them, and re-layouts  8.27 us (11%)
    pallas_call x1, Pallas kernels, on_device(): pl.pallas_call(functools.partial(kernel, (n, rows, groups, n_grp)), out_s...  66.3 us
    unnamed x17, local copies, waits for them, and re-layouts  8.27 us

profile of v1, /device:TPU:0, one launch (start us, length us, event | category | flops | bytes accessed | tf_op | source)
XLA Modules:
  0.0 75.2 jit_solution(14070561422286427063)
XLA Ops:
  0.6 0.8 %copy.10.offs = s32[9,2]{1,0:T(8,128)S(1)} copy(s32[9,2]{0,1:T(2,128)} %param.14) | data formatting | bytes 144 | tf_op args[6]
  1.4 0.0 copy-start
  1.4 1.3 %copy-done = f32[10,32,1024]{2,1,0:T(8,128)S(1)} copy-done((f32[10,32,1024]{2,1,0:T(8,128)S(1)}, f32[10,32,1024]{2,1,0:T(8,128)}, u32[]{:S(2)}) %copy-start) | copy-done | bytes 1310744
  2.7 0.0 copy-start.1
  2.7 0.9 %copy-done.1 = f32[32,1024]{1,0:T(8,128)S(1)} copy-done((f32[32,1024]{1,0:T(8,128)S(1)}, f32[32,1024]{1,0:T(8,128)}, u32[]{:S(2)}) %copy-start.1) | copy-done | bytes 131096
  3.6 0.0 copy-start.2
  3.6 0.9 %copy-done.2 = f32[32,1024]{1,0:T(8,128)S(1)} copy-done((f32[32,1024]{1,0:T(8,128)S(1)}, f32[32,1024]{1,0:T(8,128)}, u32[]{:S(2)}) %copy-start.2) | copy-done | bytes 131096
  4.5 0.0 copy-start.3
  4.5 0.7 copy-done.3
  5.2 0.0 copy-start.4
  5.2 0.7 copy-done.4
  5.9 0.0 copy-start.5
  5.9 0.7 copy-done.5
  6.6 0.0 copy-start.6
  6.6 0.7 copy-done.6
  7.2 66.3 %cycle.1 = (f32[10,32,1024]{2,1,0:T(8,128)S(1)}, f32[32,128]{1,0:T(8,128)S(1)}) custom-call(s32[9,2]{1,0:T(8,128)S(1)} %copy.10.offs, f32[9]{0:T(128)S(1)} %copy-done.6, f32[10,32,1024]{2,1,0:T(8,128)S(1)} %copy-done, f32[32,1024]{1,0:T(8,128)S(1)} %copy-done.1, f32[32,1024]{1,0:T(8,128)S(1)} %copy-done.2, s32[1,1,1024]{2,1,0:T(1,128)S(1)} %copy-done.3, ...), custom_call_target="tpu_custom_call" | custom-call | tf_op jit(solution)/shard_map/cycle/pallas_call | solution.py:509
  73.5 1.1 %copy.13 = f32[10,32,1024]{2,1,0:T(8,128)} copy(f32[10,32,1024]{2,1,0:T(8,128)S(1)} %get-tuple-element.4) | data formatting | bytes 2621440
  74.6 0.6 copy.14
Async XLA Ops:
  1.4 1.3 %copy-start = (f32[10,32,1024]{2,1,0:T(8,128)S(1)}, f32[10,32,1024]{2,1,0:T(8,128)}, u32[]{:S(2)}) copy-start(f32[10,32,1024]{2,1,0:T(8,128)} %members.1) | copy-start | bytes 3932164
  2.7 0.9 %copy-start.1 = (f32[32,1024]{1,0:T(8,128)S(1)}, f32[32,1024]{1,0:T(8,128)}, u32[]{:S(2)}) copy-start(f32[32,1024]{1,0:T(8,128)} %cx_hbm.1) | copy-start | bytes 393220
  3.6 0.9 %copy-start.2 = (f32[32,1024]{1,0:T(8,128)S(1)}, f32[32,1024]{1,0:T(8,128)}, u32[]{:S(2)}) copy-start(f32[32,1024]{1,0:T(8,128)} %cy_hbm.1) | copy-start | bytes 393220
  4.5 0.7 copy-start.3
  5.2 0.7 copy-start.4
  5.9 0.7 copy-start.5
  6.6 0.7 copy-start.6

commit v2 on v1

--- a/solution.py
+++ b/solution.py
@@ -43,10 +43,11 @@
 
 def kernel(
     shape,
-    offs, wts, members, cx_hbm, cy_hbm, cell_ref, innov_ref, weight_ref,
-    out_hbm, inc_ref,
+    offs_hbm, wts_hbm, members, cx_hbm, cy_hbm, cell_hbm, innov_hbm, weight_hbm,
+    out_hbm, inc_hbm,
     Q, C, T1, T2, D, OWN, MR, MB, MG, OBW, OBI, G0, G1,
     M0, U0, L0, M1, U1, L1, H, U, Z, ACC, XP, X0, R0, R1, NB, NM,
+    offs, wts, cell_ref, innov_ref, weight_ref, inc_buf, small_sem,
     in_sem, out_sem, hs, hr, s0, r0, s1, r1, sm1, rm1, sm2, rm2, sx0, rx0, sx1, rx1, sn, rn,
 ):
     n, rows, groups, n_grp = shape
@@ -82,6 +83,14 @@
             cols = pl.ds(b * LANES, LANES)
             yield pltpu.make_async_copy(members.at[:, :, cols], Q.at[pl.ds(0, n), b, pl.ds(top, rows)], in_sem.at[0, b])
 
+    small = [
+        pltpu.make_async_copy(a, b, small_sem.at[i])
+        for i, (a, b) in enumerate(
+            [(cell_hbm, cell_ref), (innov_hbm, innov_ref), (weight_hbm, weight_ref), (offs_hbm, offs), (wts_hbm, wts)]
+        )
+    ]
+    for copy in small:
+        copy.start()
     for copy in loads():
         copy.start()
 
@@ -210,6 +219,9 @@
     def dealt_wait(src, dst, ssem, rsem):
         for d in range(1, groups):
             remote(src.at[0], dst.at[sender(d)], ssem.at[0, d], rsem.at[0, d], at(sender(d))).wait_recv()
+
+    for copy in small:
+        copy.wait()
 
     cell = cell_ref[0]
     w = weight_ref[0]
@@ -300,7 +312,7 @@
 
     lax.fori_loop(0, n, centre, 0)
 
-    entries = offs.shape[0]
+    entries = offs.shape[1]
     weights = [wts[s] for s in range(entries)]
     weight_sum = weights[0]
     for s in range(1, entries):
@@ -332,7 +344,7 @@
                     U[c + RADIUS, b, r] = v[b]
             return c1
 
-        lax.fori_loop(0, tall // SUB, lift, 0)
+        lax.fori_loop(0, tall // SUB, lift, 0, unroll=True)
 
         def adjoint(i, c1):
             z = []
@@ -341,7 +353,7 @@
             for b in blocks:
                 acc = None
                 for s in range(entries):
-                    part = weights[s] * U[RADIUS - offs[s, 1], b, pl.ds(i * SUB + RADIUS - offs[s, 0], SUB)]
+                    part = weights[s] * U[RADIUS - offs[1, s], b, pl.ds(i * SUB + RADIUS - offs[0, s], SUB)]
                     acc = part if acc is None else acc + part
                 z.append(jnp.where(keep, acc, 0.0))
             r = pl.ds(pl.multiple_of(i * SUB, SUB), SUB)
@@ -351,19 +363,19 @@
                     Z[c + RADIUS, b, r] = v[b]
             return c1
 
-        lax.fori_loop(0, tall // SUB, adjoint, 0)
+        lax.fori_loop(0, tall // SUB, adjoint, 0, unroll=True)
 
         def direct(i, c1):
             r = pl.ds(pl.multiple_of(i * SUB, SUB), SUB)
             for b in blocks:
                 acc = None
                 for s in range(entries):
-                    part = weights[s] * Z[RADIUS + offs[s, 1], b, pl.ds(i * SUB + RADIUS + offs[s, 0], SUB)]
+                    part = weights[s] * Z[RADIUS + offs[1, s], b, pl.ds(i * SUB + RADIUS + offs[0, s], SUB)]
                     acc = part if acc is None else acc + part
                 ACC[b, r] += D[k, b, pl.ds(i * SUB + REACH, SUB)] * acc
             return c1
 
-        lax.fori_loop(0, rows // SUB, direct, 0)
+        lax.fori_loop(0, rows // SUB, direct, 0, unroll=True)
         return carry
 
     def publish(copies, dst):
@@ -420,7 +432,9 @@
         block = block + R1[b]
     NB[...] = block
     NM[me] = block
-    inc_ref[...] = block
+    inc_buf[...] = block
+    inc_copy = pltpu.make_async_copy(inc_buf, inc_hbm, small_sem.at[5])
+    inc_copy.start()
     spread_last = (NB, NM, None, None, sn, rn, False)
     spread_start(*spread_last)
 
@@ -456,6 +470,7 @@
     spread_sent(*spread_last)
     for copy in writes:
         copy.wait()
+    inc_copy.wait()
 
 
 def on_device(members, courant_x, courant_y, obs_cell, innovation, obs_weight, offsets, weights):
@@ -493,6 +508,13 @@
         vmem((groups, rows, LANES), f32),
         vmem((rows, LANES), f32),
         vmem((groups, rows, LANES), f32),
+        pltpu.SMEM((2, offsets.shape[0]), jnp.int32),
+        pltpu.SMEM(weights.shape, f32),
+        vmem(obs_cell.shape, jnp.int32),
+        vmem(innovation.shape, f32),
+        vmem(obs_weight.shape, f32),
+        vmem((rows, LANES), f32),
+        dma((6,)),
         dma((3, groups)),
         dma((groups,)),
         dma((2, n + 2)),
@@ -503,21 +525,19 @@
         dma((3, groups)),
     ]
     scratch += [dma((1, groups))] * 10
-    whole = pl.BlockSpec(memory_space=pltpu.VMEM)
-    scalar = pl.BlockSpec(memory_space=pltpu.SMEM)
-    left = pl.BlockSpec(memory_space=pl.ANY)
+    left = pl.BlockSpec(memory_space=pltpu.HBM)
     return pl.pallas_call(
         functools.partial(kernel, (n, rows, groups, n_grp)),
         out_shape=(
             jax.ShapeDtypeStruct(members.shape, f32),
             jax.ShapeDtypeStruct((rows, LANES), f32),
         ),
-        in_specs=[scalar, scalar, left, left, left, whole, whole, whole],
-        out_specs=(left, whole),
+        in_specs=[left] * 8,
+        out_specs=(left, left),
         scratch_shapes=scratch,
-        compiler_params=pltpu.CompilerParams(collective_id=0, has_side_effects=True, vmem_limit_bytes=40 << 20),
+        compiler_params=pltpu.CompilerParams(collective_id=0, has_side_effects=True, vmem_limit_bytes=67043328),
         name="cycle",
-    )(offsets, weights, members, courant_x, courant_y, obs_cell, innovation, obs_weight)
+    )(offsets.T, weights, members, courant_x, courant_y, obs_cell, innovation, obs_weight)
 
 
 def solution(mesh):

time: 75.5 us -> 55.5 us (0.74)
  Pallas kernels: 66.3 us -> 51.6 us
  local copies, waits for them, and re-layouts: 8.27 us -> 3.14 us
    pallas_call x1, Pallas kernels: 66.3 us -> 51.6 us  [on_device(): pl.pallas_call(functools.partial(kernel, (n, rows, groups, n_grp)), out_s...]
    unnamed x17 -> x4, local copies, waits for them, and re-layouts: 8.27 us -> 3.14 us
where the time goes in v2:
time: 55.5 us; the launch traced here: 55.4 us
  Pallas kernels  51.6 us (93%)
  local copies, waits for them, and re-layouts  3.14 us (6%)
  between operations  0.65 us (1%)
    pallas_call x1, Pallas kernels, on_device(): pl.pallas_call(functools.partial(kernel, (n, rows, groups, n_grp)), out_s...  51.6 us
    unnamed x4, local copies, waits for them, and re-layouts  3.14 us

profile of v2, /device:TPU:0, one launch (start us, length us, event | category | flops | bytes accessed | tf_op | source)
XLA Modules:
  0.0 55.4 jit_solution(10822312240082296218)
XLA Ops:
  0.6 51.6 %cycle.1 = (f32[10,32,1024]{2,1,0:T(8,128)}, f32[32,128]{1,0:T(8,128)}) custom-call(s32[2,9]{1,0:T(2,128)} %bitcast.1, f32[9]{0:T(128)} %wts_hbm.1, f32[10,32,1024]{2,1,0:T(8,128)} %members.1, f32[32,1024]{1,0:T(8,128)} %cx_hbm.1, f32[32,1024]{1,0:T(8,128)} %cy_hbm.1, s32[1,1,1024]{2,1,0:T(1,128)} %cell_hbm.1, f32[1,1,1024]{2,1,0:T(1,128)} %innov_hbm.1, ...), custom_call_target="tpu_custom_call" | custom-call | tf_op jit(solution)/shard_map/cycle/pallas_call | solution.py:529
  52.2 0.0 copy-start
  52.2 2.5 %copy.12 = f32[10,32,1024]{2,1,0:T(8,128)} copy(f32[10,32,1024]{2,1,0:T(8,128)} %get-tuple-element.4) | data formatting | bytes 2621440
  54.8 0.0 copy-done
  54.8 0.6 %copy.13 = f32[32,128]{1,0:T(8,128)} copy(f32[32,128]{1,0:T(8,128)S(1)} %copy-done) | data formatting | bytes 32768
Async XLA Ops:
  52.2 2.5 %copy-start = (f32[32,128]{1,0:T(8,128)S(1)}, f32[32,128]{1,0:T(8,128)}, u32[]{:S(2)}) copy-start(f32[32,128]{1,0:T(8,128)} %get-tuple-element.5) | copy-start | bytes 49156

commit v3 on v2

--- a/solution.py
+++ b/solution.py
@@ -44,10 +44,11 @@
 def kernel(
     shape,
     offs_hbm, wts_hbm, members, cx_hbm, cy_hbm, cell_hbm, innov_hbm, weight_hbm,
-    out_hbm, inc_hbm,
+    out_hbm, inc_hbm, full_hbm,
     Q, C, T1, T2, D, OWN, MR, MB, MG, OBW, OBI, G0, G1,
     M0, U0, L0, M1, U1, L1, H, U, Z, ACC, XP, X0, R0, R1, NB, NM,
     offs, wts, cell_ref, innov_ref, weight_ref, inc_buf, small_sem,
+    F, full_sem,
     in_sem, out_sem, hs, hr, s0, r0, s1, r1, sm1, rm1, sm2, rm2, sx0, rx0, sx1, rx1, sn, rn,
 ):
     n, rows, groups, n_grp = shape
@@ -107,118 +108,6 @@
     def _():
         for d in blocks:
             pl.semaphore_signal(barrier, inc=1, device_id=at(partner(d), tile + 1), device_id_type=MESH)
-
-    sides = jnp.where(has_up, 1, 0) + jnp.where(has_down, 1, 0)
-    for m in range(3):
-        @pl.when(sides == m)
-        def _(m=m):
-            pl.semaphore_wait(barrier, groups - 1 + m * groups)
-
-    for copy in loads():
-        copy.wait()
-
-    def up_copy(k):
-        return remote(
-            Q.at[k, :, pl.ds(top, SUB)], Q.at[k, :, pl.ds(top + rows, SUB)], hs.at[0, k], hr.at[0, k],
-            {"tile": tile - 1},
-        )
-
-    def down_copy(k):
-        return remote(
-            Q.at[k, :, pl.ds(top + rows - SUB, SUB)], Q.at[k, :, pl.ds(top - SUB, SUB)], hs.at[1, k], hr.at[1, k],
-            {"tile": tile + 1},
-        )
-
-    order = [n, n + 1] + list(range(n))
-    for k in order:
-        @pl.when(has_up)
-        def _(k=k):
-            up_copy(k).start()
-
-        @pl.when(has_down)
-        def _(k=k):
-            down_copy(k).start()
-
-    def halo_wait(k):
-        @pl.when(has_down)
-        def _():
-            up_copy(k).wait_recv()
-
-        @pl.when(has_up)
-        def _():
-            down_copy(k).wait_recv()
-
-    blank = jnp.zeros((SUB, LANES), jnp.float32)
-
-    @pl.when(jnp.logical_not(has_up))
-    def _():
-        for k in range(n + 2):
-            for b in blocks:
-                Q[k, b, pl.ds(top - SUB, SUB)] = blank
-        for b in blocks:
-            U0[b] = blank
-            U1[b] = blank
-
-    @pl.when(jnp.logical_not(has_down))
-    def _():
-        for k in range(n + 2):
-            for b in blocks:
-                Q[k, b, pl.ds(top + rows, SUB)] = blank
-        for b in blocks:
-            L0[b] = blank
-            L1[b] = blank
-
-    def spread_start(src, main, up, low, ssem, rsem, edges):
-        for d in range(1, groups):
-            remote(src, main.at[me], ssem.at[0, d], rsem.at[0, d], at(partner(d))).start()
-        if edges:
-            @pl.when(has_up)
-            def _():
-                for d in blocks:
-                    remote(src.at[pl.ds(0, SUB)], low.at[me], ssem.at[1, d], rsem.at[1, d], at(partner(d), tile - 1)).start()
-
-            @pl.when(has_down)
-            def _():
-                for d in blocks:
-                    remote(src.at[pl.ds(rows - SUB, SUB)], up.at[me], ssem.at[2, d], rsem.at[2, d], at(partner(d), tile + 1)).start()
-
-    def spread_recv(src, main, up, low, ssem, rsem, edges):
-        for d in range(1, groups):
-            remote(src, main.at[sender(d)], ssem.at[0, d], rsem.at[0, d], at(sender(d))).wait_recv()
-        if edges:
-            @pl.when(has_down)
-            def _():
-                for d in blocks:
-                    remote(src.at[pl.ds(0, SUB)], low.at[sender(d)], ssem.at[1, d], rsem.at[1, d], at(sender(d))).wait_recv()
-
-            @pl.when(has_up)
-            def _():
-                for d in blocks:
-                    remote(src.at[pl.ds(0, SUB)], up.at[sender(d)], ssem.at[2, d], rsem.at[2, d], at(sender(d))).wait_recv()
-
-    def spread_sent(src, main, up, low, ssem, rsem, edges):
-        for d in range(1, groups):
-            remote(src, main.at[me], ssem.at[0, d], rsem.at[0, d], at(partner(d))).wait_send()
-        if edges:
-            @pl.when(has_up)
-            def _():
-                for d in blocks:
-                    remote(src.at[pl.ds(0, SUB)], low.at[me], ssem.at[1, d], rsem.at[1, d], at(partner(d), tile - 1)).wait_send()
-
-            @pl.when(has_down)
-            def _():
-                for d in blocks:
-                    remote(src.at[pl.ds(0, SUB)], up.at[me], ssem.at[2, d], rsem.at[2, d], at(partner(d), tile + 1)).wait_send()
-
-    def deal(src, dst, ssem, rsem):
-        return [
-            remote(src.at[partner(d)], dst.at[me], ssem.at[0, d], rsem.at[0, d], at(partner(d)))
-            for d in range(1, groups)
-        ]
-
-    def dealt_wait(src, dst, ssem, rsem):
-        for d in range(1, groups):
-            remote(src.at[0], dst.at[sender(d)], ssem.at[0, d], rsem.at[0, d], at(sender(d))).wait_recv()
 
     for copy in small:
         copy.wait()
@@ -240,8 +129,122 @@
     OBI[...] = both[rows:]
     G0[...] = both[rows:]
     M0[me] = both[rows:]
+
+    sides = jnp.where(has_up, 1, 0) + jnp.where(has_down, 1, 0)
+    for m in range(3):
+        @pl.when(sides == m)
+        def _(m=m):
+            pl.semaphore_wait(barrier, groups - 1 + m * groups)
+
+
+    def up_copy(k):
+        return remote(
+            Q.at[k, :, pl.ds(top, SUB)], Q.at[k, :, pl.ds(top + rows, SUB)], hs.at[0, k], hr.at[0, k],
+            {"tile": tile - 1},
+        )
+
+    def down_copy(k):
+        return remote(
+            Q.at[k, :, pl.ds(top + rows - SUB, SUB)], Q.at[k, :, pl.ds(top - SUB, SUB)], hs.at[1, k], hr.at[1, k],
+            {"tile": tile + 1},
+        )
+
+    def halo_wait(k):
+        @pl.when(has_down)
+        def _():
+            up_copy(k).wait_recv()
+
+        @pl.when(has_up)
+        def _():
+            down_copy(k).wait_recv()
+
+    blank = jnp.zeros((SUB, LANES), jnp.float32)
+
+    @pl.when(jnp.logical_not(has_up))
+    def _():
+        for k in range(n + 2):
+            for b in blocks:
+                Q[k, b, pl.ds(top - SUB, SUB)] = blank
+        for b in blocks:
+            U0[b] = blank
+            U1[b] = blank
+
+    @pl.when(jnp.logical_not(has_down))
+    def _():
+        for k in range(n + 2):
+            for b in blocks:
+                Q[k, b, pl.ds(top + rows, SUB)] = blank
+        for b in blocks:
+            L0[b] = blank
+            L1[b] = blank
+
+    def spread_start(src, main, up, low, ssem, rsem, edges):
+        for d in range(1, groups):
+            remote(src, main.at[me], ssem.at[0, d], rsem.at[0, d], at(partner(d))).start()
+        if edges:
+            @pl.when(has_up)
+            def _():
+                for d in blocks:
+                    remote(src.at[pl.ds(0, SUB)], low.at[me], ssem.at[1, d], rsem.at[1, d], at(partner(d), tile - 1)).start()
+
+            @pl.when(has_down)
+            def _():
+                for d in blocks:
+                    remote(src.at[pl.ds(rows - SUB, SUB)], up.at[me], ssem.at[2, d], rsem.at[2, d], at(partner(d), tile + 1)).start()
+
+    def spread_recv(src, main, up, low, ssem, rsem, edges):
+        for d in range(1, groups):
+            remote(src, main.at[sender(d)], ssem.at[0, d], rsem.at[0, d], at(sender(d))).wait_recv()
+        if edges:
+            @pl.when(has_down)
+            def _():
+                for d in blocks:
+                    remote(src.at[pl.ds(0, SUB)], low.at[sender(d)], ssem.at[1, d], rsem.at[1, d], at(sender(d))).wait_recv()
+
+            @pl.when(has_up)
+            def _():
+                for d in blocks:
+                    remote(src.at[pl.ds(0, SUB)], up.at[sender(d)], ssem.at[2, d], rsem.at[2, d], at(sender(d))).wait_recv()
+
+    def spread_sent(src, main, up, low, ssem, rsem, edges):
+        for d in range(1, groups):
+            remote(src, main.at[me], ssem.at[0, d], rsem.at[0, d], at(partner(d))).wait_send()
+        if edges:
+            @pl.when(has_up)
+            def _():
+                for d in blocks:
+                    remote(src.at[pl.ds(0, SUB)], low.at[me], ssem.at[1, d], rsem.at[1, d], at(partner(d), tile - 1)).wait_send()
+
+            @pl.when(has_down)
+            def _():
+                for d in blocks:
+                    remote(src.at[pl.ds(0, SUB)], up.at[me], ssem.at[2, d], rsem.at[2, d], at(partner(d), tile + 1)).wait_send()
+
+    def deal(src, dst, ssem, rsem):
+        return [
+            remote(src.at[partner(d)], dst.at[me], ssem.at[0, d], rsem.at[0, d], at(partner(d)))
+            for d in range(1, groups)
+        ]
+
+    def dealt_wait(src, dst, ssem, rsem):
+        for d in range(1, groups):
+            remote(src.at[0], dst.at[sender(d)], ssem.at[0, d], rsem.at[0, d], at(sender(d))).wait_recv()
+
     spread0 = (G0, M0, U0, L0, s0, r0, True)
     spread_start(*spread0)
+    for copy in loads():
+        copy.wait()
+
+    order = [n, n + 1] + list(range(n))
+    for k in order:
+        @pl.when(has_up)
+        def _(k=k):
+            up_copy(k).start()
+
+        @pl.when(has_down)
+        def _(k=k):
+            down_copy(k).start()
+
 
     halo_wait(n)
     halo_wait(n + 1)
@@ -294,9 +297,16 @@
             for b in blocks:
                 D[k, b, r] = new[b]
                 OWN[b, r] += new[b] * (1.0 / n)
+        for b in blocks:
+            F[k, b] = D[k, b, pl.ds(REACH, rows)]
         return carry
 
     lax.fori_loop(0, n, forecast, 0)
+    writes = [
+        pltpu.make_async_copy(F.at[:, b], out_hbm.at[:, :, pl.ds(b * LANES, LANES)], out_sem.at[b]) for b in blocks
+    ]
+    for copy in writes:
+        copy.start()
 
     mean_out = deal(OWN, MR, sm1, rm1)
     for copy in mean_out:
@@ -448,27 +458,18 @@
             down_copy(k).wait_send()
 
     spread_recv(*spread_last)
-    writes = []
-    for b in blocks:
-        base = OWN[b, pl.ds(REACH, rows)] + NM[b]
-
-        def finish(k, carry, b=b, base=base):
-            Q[k, b, pl.ds(top, rows)] = D[k, b, pl.ds(REACH, rows)] + base
-            return carry
-
-        lax.fori_loop(0, n, finish, 0)
-        copy = pltpu.make_async_copy(
-            Q.at[pl.ds(0, n), b, pl.ds(top, rows)], out_hbm.at[:, :, pl.ds(b * LANES, LANES)], out_sem.at[b]
-        )
+    fulls = [
+        pltpu.make_async_copy(NM.at[b], full_hbm.at[:, pl.ds(b * LANES, LANES)], full_sem.at[b]) for b in blocks
+    ]
+    for copy in fulls:
         copy.start()
-        writes.append(copy)
     spread_sent(*spread0)
     for copy in mean_out + second_out:
         copy.wait_send()
     spread_sent(*spread_mean)
     spread_sent(*spread1)
     spread_sent(*spread_last)
-    for copy in writes:
+    for copy in writes + fulls:
         copy.wait()
     inc_copy.wait()
 
@@ -515,6 +516,8 @@
         vmem(obs_weight.shape, f32),
         vmem((rows, LANES), f32),
         dma((6,)),
+        vmem((n, groups, rows, LANES), f32),
+        dma((groups,)),
         dma((3, groups)),
         dma((groups,)),
         dma((2, n + 2)),
@@ -526,18 +529,20 @@
     ]
     scratch += [dma((1, groups))] * 10
     left = pl.BlockSpec(memory_space=pltpu.HBM)
-    return pl.pallas_call(
+    fields, block, full = pl.pallas_call(
         functools.partial(kernel, (n, rows, groups, n_grp)),
         out_shape=(
             jax.ShapeDtypeStruct(members.shape, f32),
             jax.ShapeDtypeStruct((rows, LANES), f32),
+            jax.ShapeDtypeStruct((rows, cols), f32),
         ),
         in_specs=[left] * 8,
-        out_specs=(left, left),
+        out_specs=(left, left, left),
         scratch_shapes=scratch,
         compiler_params=pltpu.CompilerParams(collective_id=0, has_side_effects=True, vmem_limit_bytes=67043328),
         name="cycle",
     )(offsets.T, weights, members, courant_x, courant_y, obs_cell, innovation, obs_weight)
+    return fields + full[None], block
 
 
 def solution(mesh):

time: 55.5 us -> 55.4 us (level)
  other arithmetic: 0 us -> 2.55 us
  local copies, waits for them, and re-layouts: 3.14 us -> 0.61 us
    add x0 -> x1, other arithmetic: none -> 2.55 us  [on_device(): return (fields + full[None], block)]
    unnamed x4 -> x3, local copies, waits for them, and re-layouts: 3.14 us -> 0.61 us
where the time goes in v3:
time: 55.4 us; the launch traced here: 55.3 us
  Pallas kernels  51.5 us (93%)
  other arithmetic  2.55 us (5%)
  between operations  0.65 us (1%)
  local copies, waits for them, and re-layouts  0.61 us (1%)
    pallas_call x1, Pallas kernels, on_device(): pl.pallas_call(functools.partial(kernel, (n, rows, groups, n_grp)), out_s...  51.5 us
    add x1, other arithmetic, on_device(): return (fields + full[None], block)  2.55 us

profile of v3, /device:TPU:0, one launch (start us, length us, event | category | flops | bytes accessed | tf_op | source)
XLA Modules:
  0.0 55.3 jit_solution(15081632526890283112)
XLA Ops:
  0.6 51.5 %cycle.1 = (f32[10,32,1024]{2,1,0:T(8,128)}, f32[32,128]{1,0:T(8,128)}, f32[32,1024]{1,0:T(8,128)}) custom-call(s32[2,9]{1,0:T(2,128)} %bitcast.1, f32[9]{0:T(128)} %wts_hbm.1, f32[10,32,1024]{2,1,0:T(8,128)} %members.1, f32[32,1024]{1,0:T(8,128)} %cx_hbm.1, f32[32,1024]{1,0:T(8,128)} %cy_hbm.1, s32[1,1,1024]{2,1,0:T(1,128)} %cell_hbm.1, ...), custom_call_target="tpu_custom_call" | custom-call | tf_op jit(solution)/shard_map/cycle/pallas_call | solution.py:532
  52.1 0.0 copy-start
  52.1 2.5 %broadcast_add_fusion = f32[10,32,1024]{2,1,0:T(8,128)} fusion(f32[10,32,1024]{2,1,0:T(8,128)} %get-tuple-element.5, f32[32,1024]{1,0:T(8,128)} %get-tuple-element.6), kind=kLoop, calls=%fused_computation | loop fusion | flops 327680 | bytes 2752512 | tf_op jit(solution)/shard_map/add | solution.py:545
  54.7 0.0 copy-done
  54.7 0.6 %copy.11 = f32[32,128]{1,0:T(8,128)} copy(f32[32,128]{1,0:T(8,128)S(1)} %copy-done) | data formatting | bytes 32768
Async XLA Ops:
  52.1 2.6 %copy-start = (f32[32,128]{1,0:T(8,128)S(1)}, f32[32,128]{1,0:T(8,128)}, u32[]{:S(2)}) copy-start(f32[32,128]{1,0:T(8,128)} %get-tuple-element.11) | copy-start | bytes 49156

commit v4 on v3

--- a/solution.py
+++ b/solution.py
@@ -266,62 +266,6 @@
         for b in blocks:
             OWN[b, pl.ds(i * SUB, SUB)] = blank
 
-    def advect(get, first, i):
-        base = first + i * SUB
-        q = [get(b, base) for b in blocks]
-        before = moved(q, -1, lane)
-        after = moved(q, 1, lane)
-        out = []
-        for b in blocks:
-            r = pl.ds(base, SUB)
-            out.append(
-                (C[0, b, r] * q[b] + C[1, b, r] * get(b, base - 1))
-                + (C[2, b, r] * get(b, base + 1) + C[3, b, r] * before[b])
-                + C[4, b, r] * after[b]
-            )
-        return out
-
-    def forecast(k, carry):
-        halo_wait(k)
-        for i in range(rows // SUB + 2):
-            new = advect(lambda b, r: Q[k, b, pl.ds(r, SUB)], top - SUB, i)
-            for b in blocks:
-                T1[b, pl.ds(top - SUB + i * SUB, SUB)] = new[b]
-        for i in range(rows // SUB + 2):
-            new = advect(lambda b, r: T1[b, pl.ds(r, SUB)], top - SUB, i)
-            for b in blocks:
-                T2[b, pl.ds(top - SUB + i * SUB, SUB)] = new[b]
-        for i in range(tall // SUB):
-            new = advect(lambda b, r: T2[b, pl.ds(r, SUB)], top - REACH, i)
-            r = pl.ds(i * SUB, SUB)
-            for b in blocks:
-                D[k, b, r] = new[b]
-                OWN[b, r] += new[b] * (1.0 / n)
-        for b in blocks:
-            F[k, b] = D[k, b, pl.ds(REACH, rows)]
-        return carry
-
-    lax.fori_loop(0, n, forecast, 0)
-    writes = [
-        pltpu.make_async_copy(F.at[:, b], out_hbm.at[:, :, pl.ds(b * LANES, LANES)], out_sem.at[b]) for b in blocks
-    ]
-    for copy in writes:
-        copy.start()
-
-    mean_out = deal(OWN, MR, sm1, rm1)
-    for copy in mean_out:
-        copy.start()
-    MR[me] = OWN[me]
-
-    def centre(k, carry):
-        for i in range(tall // SUB):
-            r = pl.ds(i * SUB, SUB)
-            for b in blocks:
-                D[k, b, r] = D[k, b, r] - OWN[b, r]
-        return carry
-
-    lax.fori_loop(0, n, centre, 0)
-
     entries = offs.shape[1]
     weights = [wts[s] for s in range(entries)]
     weight_sum = weights[0]
@@ -375,6 +319,8 @@
 
         lax.fori_loop(0, tall // SUB, adjoint, 0, unroll=True)
 
+        sign = jnp.where(k == n, -1.0, 1.0)
+
         def direct(i, c1):
             r = pl.ds(pl.multiple_of(i * SUB, SUB), SUB)
             for b in blocks:
@@ -382,7 +328,7 @@
                 for s in range(entries):
                     part = weights[s] * Z[RADIUS + offs[1, s], b, pl.ds(i * SUB + RADIUS + offs[0, s], SUB)]
                     acc = part if acc is None else acc + part
-                ACC[b, r] += D[k, b, pl.ds(i * SUB + REACH, SUB)] * acc
+                ACC[b, r] += (sign * D[k, b, pl.ds(i * SUB + REACH, SUB)]) * acc
             return c1
 
         lax.fori_loop(0, rows // SUB, direct, 0, unroll=True)
@@ -397,11 +343,79 @@
             copy.start()
         dst[me] = XP[me]
 
+    def advect(get, first, i):
+        base = first + i * SUB
+        q = [get(b, base) for b in blocks]
+        before = moved(q, -1, lane)
+        after = moved(q, 1, lane)
+        out = []
+        for b in blocks:
+            r = pl.ds(base, SUB)
+            out.append(
+                (C[0, b, r] * q[b] + C[1, b, r] * get(b, base - 1))
+                + (C[2, b, r] * get(b, base + 1) + C[3, b, r] * before[b])
+                + C[4, b, r] * after[b]
+            )
+        return out
+
+    def forecast(k, carry):
+        halo_wait(k)
+        for i in range(rows // SUB + 2):
+            new = advect(lambda b, r: Q[k, b, pl.ds(r, SUB)], top - SUB, i)
+            for b in blocks:
+                T1[b, pl.ds(top - SUB + i * SUB, SUB)] = new[b]
+        for i in range(rows // SUB + 2):
+            new = advect(lambda b, r: T1[b, pl.ds(r, SUB)], top - SUB, i)
+            for b in blocks:
+                T2[b, pl.ds(top - SUB + i * SUB, SUB)] = new[b]
+        for i in range(tall // SUB):
+            new = advect(lambda b, r: T2[b, pl.ds(r, SUB)], top - REACH, i)
+            r = pl.ds(i * SUB, SUB)
+            for b in blocks:
+                D[k, b, r] = new[b]
+        for b in blocks:
+            F[k, b] = D[k, b, pl.ds(REACH, rows)]
+        for i in range(tall // SUB):
+            r = pl.ds(i * SUB, SUB)
+            for b in blocks:
+                gap = D[k, b, r] - D[0, b, r]
+                D[k, b, r] = jnp.where(k > 0, gap, D[k, b, r])
+                OWN[b, r] += gap * (1.0 / n)
+        return carry
+
+    lax.fori_loop(0, 2, forecast, 0)
     spread_recv(*spread0)
     assemble(M0, U0, L0)
     clear()
-    half = n // 2
-    lax.fori_loop(0, half, apply, 0)
+    steps = (n - 2) // 3
+
+    def both_stages(j, carry):
+        lax.fori_loop(3 * j + 2, 3 * j + 5, forecast, 0)
+        return apply(j + 1, carry)
+
+    lax.fori_loop(0, steps, both_stages, 0)
+    lax.fori_loop(3 * steps + 2, n, forecast, 0)
+    for i in range(tall // SUB):
+        r = pl.ds(i * SUB, SUB)
+        for b in blocks:
+            gap = OWN[b, r]
+            D[n, b, r] = gap * math.sqrt(n)
+            OWN[b, r] = gap + D[0, b, r]
+    writes = [
+        pltpu.make_async_copy(F.at[:, b], out_hbm.at[:, :, pl.ds(b * LANES, LANES)], out_sem.at[b]) for b in blocks
+    ]
+    for copy in writes:
+        copy.start()
+
+    mean_out = deal(OWN, MR, sm1, rm1)
+    for copy in mean_out:
+        copy.start()
+    MR[me] = OWN[me]
+
+    for b in blocks:
+        D[n + 1, b] = jnp.full((tall, LANES), math.sqrt((total - 1) / groups), jnp.float32)
+    half = (steps + 1 + n + 2) // 2
+    lax.fori_loop(steps + 1, half, apply, 0)
     dealt_wait(OWN, MR, sm1, rm1)
     mean = MR[0]
     for b in range(1, groups):
@@ -410,12 +424,11 @@
     MG[me] = mean * (1.0 / groups)
     spread_mean = (MB, MG, None, None, sm2, rm2, False)
     spread_start(*spread_mean)
-    lax.fori_loop(half, n, apply, 0)
+    lax.fori_loop(half, n + 2, apply, 0)
     spread_recv(*spread_mean)
     for b in blocks:
-        D[n, b] = (OWN[b] - MG[b]) * math.sqrt(n)
-        D[n + 1, b] = jnp.full((tall, LANES), math.sqrt((total - 1) / groups), jnp.float32)
-    lax.fori_loop(n, n + 2, apply, 0)
+        D[n + 2, b] = (OWN[b] - MG[b]) * math.sqrt(n)
+    lax.fori_loop(n + 2, n + 3, apply, 0)
     first_out = deal(XP, R0, sx0, rx0)
     publish(first_out, R0)
     dealt_wait(XP, R0, sx0, rx0)
@@ -433,7 +446,7 @@
     spread_recv(*spread1)
     assemble(M1, U1, L1)
     clear()
-    lax.fori_loop(0, n + 2, apply, 0)
+    lax.fori_loop(1, n + 3, apply, 0)
     second_out = deal(XP, R1, sx1, rx1)
     publish(second_out, R1)
     dealt_wait(XP, R1, sx1, rx1)
@@ -489,7 +502,7 @@
         vmem((5, groups, deep, LANES), f32),
         vmem((groups, deep, LANES), f32),
         vmem((groups, deep, LANES), f32),
-        vmem((n + 2, groups, tall, LANES), f32),
+        vmem((n + 3, groups, tall, LANES), f32),
         vmem((groups, tall, LANES), f32),
         vmem((groups, tall, LANES), f32),
         vmem((tall, LANES), f32),

time: 55.4 us -> 56.7 us (1.023)
  Pallas kernels: 51.5 us -> 52.8 us
    pallas_call x1, Pallas kernels: 51.5 us -> 52.8 us  [on_device(): pl.pallas_call(functools.partial(kernel, (n, rows, groups, n_grp)), out_s...]
where the time goes in v4:
time: 56.7 us; the launch traced here: 56.6 us
  Pallas kernels  52.8 us (93%)
  other arithmetic  2.55 us (4%)
  between operations  0.65 us (1%)
  local copies, waits for them, and re-layouts  0.61 us (1%)
    pallas_call x1, Pallas kernels, on_device(): pl.pallas_call(functools.partial(kernel, (n, rows, groups, n_grp)), out_s...  52.8 us
    add x1, other arithmetic, on_device(): return (fields + full[None], block)  2.55 us

profile of v4, /device:TPU:0, one launch (start us, length us, event | category | flops | bytes accessed | tf_op | source)
XLA Modules:
  0.0 56.6 jit_solution(17456433230685771146)
XLA Ops:
  0.6 52.8 %cycle.1 = (f32[10,32,1024]{2,1,0:T(8,128)}, f32[32,128]{1,0:T(8,128)}, f32[32,1024]{1,0:T(8,128)}) custom-call(s32[2,9]{1,0:T(2,128)} %bitcast.1, f32[9]{0:T(128)} %wts_hbm.1, f32[10,32,1024]{2,1,0:T(8,128)} %members.1, f32[32,1024]{1,0:T(8,128)} %cx_hbm.1, f32[32,1024]{1,0:T(8,128)} %cy_hbm.1, s32[1,1,1024]{2,1,0:T(1,128)} %cell_hbm.1, ...), custom_call_target="tpu_custom_call" | custom-call | tf_op jit(solution)/shard_map/cycle/pallas_call | solution.py:545
  53.4 0.0 copy-start
  53.4 2.5 %broadcast_add_fusion = f32[10,32,1024]{2,1,0:T(8,128)} fusion(f32[10,32,1024]{2,1,0:T(8,128)} %get-tuple-element.5, f32[32,1024]{1,0:T(8,128)} %get-tuple-element.6), kind=kLoop, calls=%fused_computation | loop fusion | flops 327680 | bytes 2752512 | tf_op jit(solution)/shard_map/add | solution.py:558
  56.0 0.0 copy-done
  56.0 0.6 %copy.11 = f32[32,128]{1,0:T(8,128)} copy(f32[32,128]{1,0:T(8,128)S(1)} %copy-done) | data formatting | bytes 32768
Async XLA Ops:
  53.4 2.6 %copy-start = (f32[32,128]{1,0:T(8,128)S(1)}, f32[32,128]{1,0:T(8,128)}, u32[]{:S(2)}) copy-start(f32[32,128]{1,0:T(8,128)} %get-tuple-element.11) | copy-start | bytes 49156
